TPU v7x, 32 devices: a whole 2x2x4 slice. The times are simulated.
32 devices in a mesh: gx: 4 (over y, x), gy: 8 (over z, core).
Axes of the slice: x: 2, y: 2, z: 4, core: 2. Of those that a mesh axis runs over, the one named last changes fastest.
Arguments:
- tokens: bfloat16 [512, 16384], P(None, ('gx', 'gy')), may hold values from -6 to 6
- gate_weight: bfloat16 [16384, 26624], P('gx', 'gy'), may hold values from -0.046875 to 0.046875
- up_weight: bfloat16 [16384, 26624], P('gx', 'gy'), may hold values from -0.046875 to 0.046875
- down_weight: bfloat16 [26624, 16384], P('gy', 'gx'), may hold values from -0.0390625 to 0.0390625
- mixing: float32 [52, 52], replicated, may hold values from -0.3 to 1.2
Outputs:
- mixed: bfloat16 [512, 16384], P(None, ('gx', 'gy'))
All inputs are finite; a program needn't handle non-finite values.
Results may differ from a plain program's by a relative error of at most 0.025.
Values may be sent and summed in bfloat16 or wider, within the bound.
A program may use at most 192 MiB of HBM per device.

v0:
```python
import jax
import jax.numpy as jnp
from jax import lax
from jax.sharding import PartitionSpec as P


def parity_sign(values):
    ones_count = jnp.zeros_like(values)
    for bit_place in range(20):
        ones_count = ones_count + jnp.bitwise_and(jnp.right_shift(values, bit_place), 1)
    return (1 - 2 * jnp.bitwise_and(ones_count, 1)).astype(jnp.float32)


def sylvester(matrix_order):
    indices = jnp.arange(matrix_order, dtype=jnp.int32)
    common = jnp.bitwise_and(indices[:, None], indices[None, :])
    return parity_sign(common)


def mix_across(hidden):
    position = lax.axis_index("gy")
    segment = lax.all_gather(hidden[None], "gy", axis=0, tiled=True)
    indices = jnp.arange(segment.shape[0], dtype=jnp.int32)
    common = jnp.bitwise_and(indices, position)
    sign_row = parity_sign(common)
    return jnp.tensordot(sign_row, segment.astype(jnp.float32), axes=1)


def on_device(tokens, gate_weight, up_weight, down_weight, mixing):
    col_block = gate_weight.shape[1]
    a_points = mixing.shape[0]
    inner_size = col_block // a_points
    factor = 1.0 / jnp.sqrt(jnp.float32(inner_size * lax.axis_size("gy")))
    highest = lax.Precision.HIGHEST
    segment = lax.all_gather(tokens, "gy", axis=1, tiled=True)
    partial_value = jnp.stack(
        [
            jnp.dot(segment, gate_weight, preferred_element_type=jnp.float32),
            jnp.dot(segment, up_weight, preferred_element_type=jnp.float32),
        ],
        axis=1,
    )
    summed = lax.psum_scatter(partial_value, "gx", scatter_dimension=0, tiled=True)
    hidden = (jax.nn.silu(summed[:, 0]) * summed[:, 1]).astype(jnp.bfloat16)
    blended = mix_across(hidden)
    row_count = blended.shape[0]
    section_one = jnp.einsum(
        "tba,ad->tbd", blended.reshape(row_count, inner_size, a_points), mixing, precision=highest
    )
    section_two = jnp.einsum("tbd,bc->tcd", section_one, sylvester(inner_size), precision=highest)
    rotated = (section_two * factor).astype(jnp.bfloat16).reshape(row_count, col_block)
    all_rows = lax.all_gather(rotated, "gx", axis=0, tiled=True)
    products = jnp.dot(all_rows, down_weight, preferred_element_type=jnp.float32)
    return lax.psum_scatter(products.astype(jnp.bfloat16), "gy", scatter_dimension=1, tiled=True)


def solution(mesh):
    placed = (P(None, ("gx", "gy")), P("gx", "gy"), P("gx", "gy"), P("gy", "gx"), P())
    return jax.shard_map(
        on_device, mesh=mesh, in_specs=placed, out_specs=P(None, ("gx", "gy")), check_vma=False
    )
```

profile of v0, /device:TPU:0, one launch (start us, length us, event | category | flops | bytes accessed | tf_op | source)
XLA Modules:
  0.0 461.7 jit_solution(8941715812542117240)
XLA Ops:
  6.5 0.0 copy-start
  6.5 0.0 all-gather.4.cloned.1.call-start
  6.5 0.7 all-gather.4.cloned.1.call-update
  7.3 0.0 reduce-scatter.3.cloned.1.call-start
  7.3 51.3 %all-gather.4.cloned.1.call-done = bf16[512,4096]{1,0:T(8,128)(2,1)} async-done(((bf16[512,512]{1,0:T(8,128)(2,1)}), bf16[512,4096]{1,0:T(8,128)(2,1)}) %all-gather.4.cloned.1.call-update) | async-done | bytes 4194320 | tf_op jit(solution)/shard_map/all_gather | solution.py:35
  58.6 0.0 copy-start.1
  58.6 27.3 %convolution_bitcast_fusion = f32[512,1,3328]{2,0,1:T(8,128)} fusion(bf16[512,4096]{1,0:T(8,128)(2,1)} %all-gather.4.cloned.1.call-done, bf16[4096,3328]{1,0:T(8,128)(2,1)} %param.7), kind=kOutput, calls=%fused_computation.3 | convolution fusion | flops 13958643712 | bytes 38273024 | tf_op jit(solution)/shard_map/dot_general | solution.py:39
  85.9 0.0 copy-done.1
  85.9 22.3 %convolution_bitcast_fusion.1 = f32[512,1,3328]{2,0,1:T(8,128)} fusion(bf16[512,4096]{1,0:T(8,128)(2,1)S(1)} %copy-done.1, bf16[4096,3328]{1,0:T(8,128)(2,1)} %param.6), kind=kOutput, calls=%fused_computation.4 | convolution fusion | flops 13958643712 | bytes 38273024 | tf_op jit(solution)/shard_map/dot_general | solution.py:38
  108.2 10.7 %pad_maximum_fusion = f32[512,2,3328]{2,0,1:T(8,128)} fusion(f32[512,1,3328]{2,0,1:T(8,128)} %convolution_bitcast_fusion, f32[512,1,3328]{2,0,1:T(8,128)} %convolution_bitcast_fusion.1), kind=kLoop, calls=%fused_computation | loop fusion | flops 3407872 | bytes 27262976 | tf_op jit(solution)/shard_map/stack | solution.py:36
  118.9 0.0 reduce-scatter.3.cloned.1.call-update
  118.9 0.0 all-gather.6.cloned.1.call-start
  118.9 128.1 %reduce-scatter.3.cloned.1.call-done = f32[128,2,3328]{2,0,1:T(8,128)} async-done(((f32[512,2,3328]{2,0,1:T(8,128)}), f32[128,2,3328]{2,0,1:T(8,128)}) %reduce-scatter.3.cloned.1.call-update) | async-done | bytes 3407888 | tf_op jit(solution)/shard_map/reduce_scatter | solution.py:43
  247.0 3.3 fusion.3
  250.4 0.0 all-gather.6.cloned.1.call-update
  250.4 0.0 all-gather.8.cloned.1.call-start
  250.4 69.1 %all-gather.6.cloned.1.call-done = bf16[8,128,3328]{2,1,0:T(8,128)(2,1)} async-done(((bf16[1,128,3328]{2,1,0:T(8,128)(2,1)}), bf16[8,128,3328]{2,1,0:T(8,128)(2,1)}) %all-gather.6.cloned.1.call-update) | async-done | bytes 6815760 | tf_op jit(solution)/shard_map/all_gather | solution.py:22
  319.5 9.0 %fusion = f32[1,128,3328]{2,0,1:T(1,128)S(1)} fusion(bf16[8,128,3328]{2,1,0:T(8,128)(2,1)} %all-gather.6.cloned.1.call-done, s32[]{:T(128)S(6)} %axis_index.12), kind=kOutput, calls=%fused_computation.1 | convolution fusion | flops 6816256 | bytes 8519684 | tf_op jit(solution)/shard_map/dot_general | solution.py:26
  328.6 3.3 copy.11
  331.9 1.5 reshape.47
  333.3 0.0 copy-done
  333.3 1.7 fusion.78
  335.1 1.8 fusion.8
  336.8 0.6 copy.9
  337.4 1.1 reshape.48
  338.5 0.0 all-gather.8.cloned.1.call-update
  338.5 0.0 reduce-scatter.5.cloned.1.call-start
  338.6 44.6 %all-gather.8.cloned.1.call-done = bf16[512,3328]{0,1:T(8,128)(2,1)} async-done(((bf16[128,3328]{0,1:T(8,128)(2,1)}), bf16[512,3328]{0,1:T(8,128)(2,1)}) %all-gather.8.cloned.1.call-update) | async-done | bytes 3407888 | tf_op jit(solution)/shard_map/all_gather | solution.py:52
  383.2 21.9 %convolution_convert_fusion = bf16[512,4096]{1,0:T(8,128)(2,1)} fusion(bf16[512,3328]{0,1:T(8,128)(2,1)} %all-gather.8.cloned.1.call-done, bf16[3328,4096]{1,0:T(8,128)(2,1)} %param.8), kind=kOutput, calls=%fused_computation.5 | convolution fusion | flops 13960740864 | bytes 34865152 | tf_op jit(solution)/shard_map/dot_general | solution.py:53
  405.0 0.0 reduce-scatter.5.cloned.1.call-update
  405.1 50.1 %reduce-scatter.5.cloned.1.call-done = bf16[512,512]{1,0:T(8,128)(2,1)} async-done(((bf16[512,4096]{1,0:T(8,128)(2,1)}), bf16[512,512]{1,0:T(8,128)(2,1)}) %reduce-scatter.5.cloned.1.call-update) | async-done | bytes 524304 | tf_op jit(solution)/shard_map/reduce_scatter | solution.py:54
Async XLA Ops:
  6.5 326.8 %copy-start = (f32[52,52]{1,0:T(8,128)S(1)}, f32[52,52]{1,0:T(8,128)}, u32[]{:S(2)}) copy-start(f32[52,52]{1,0:T(8,128)} %param.9) | copy-start | bytes 32452
  6.5 52.0 %all-gather.4.cloned.1.call-start = ((), (), s32[]{:S(2)}) async-start(), calls=%async_computation.2 | async-start | bytes 4718592 | tf_op jit(solution)/shard_map/all_gather | solution.py:35
  7.3 239.8 %reduce-scatter.3.cloned.1.call-start = ((), (), s32[]{:S(2)}) async-start(), calls=%async_computation.3 | async-start | bytes 17039360 | tf_op jit(solution)/shard_map/reduce_scatter | solution.py:43
  58.6 27.3 %copy-start.1 = (bf16[512,4096]{1,0:T(8,128)(2,1)S(1)}, bf16[512,4096]{1,0:T(8,128)(2,1)}, u32[]{:S(2)}) copy-start(bf16[512,4096]{1,0:T(8,128)(2,1)} %all-gather.4.cloned.1.call-done) | copy-start | bytes 12582916
  118.9 200.7 %all-gather.6.cloned.1.call-start = ((), (), s32[]{:S(2)}) async-start(), calls=%async_computation.4 | async-start | bytes 7667712 | tf_op jit(solution)/shard_map/all_gather | solution.py:22
  250.4 132.8 %all-gather.8.cloned.1.call-start = ((), (), s32[]{:S(2)}) async-start(), calls=%async_computation.5 | async-start | bytes 4259840 | tf_op jit(solution)/shard_map/all_gather | solution.py:52
  338.5 116.6 %reduce-scatter.5.cloned.1.call-start = ((), (), s32[]{:S(2)}) async-start(), calls=%async_computation.6 | async-start | bytes 4718592 | tf_op jit(solution)/shard_map/reduce_scatter | solution.py:54
Sparse Core Ops, SparseCore 0:
  8.9 49.5 all-gather.3
  119.0 127.9 reduce-scatter.2
  250.5 69.0 all-gather.5
  338.6 44.4 all-gather.7
  405.2 49.8 reduce-scatter.4
where the time goes:
time: 462 us
  waiting for transfers between devices  344 us (74%)
  matrix products  84 us (18%)
  other arithmetic  14 us (3%)
  between operations  13.2 us (3%)
  local copies, waits for them, and re-layouts  6.42 us (1%)
    reduce_scatter x1, waiting for transfers between devices, on_device(): lax.psum_scatter(partial_value, 'gx', scatter_dimension=0, tiled=True)  128 us
    all_gather x1, waiting for transfers between devices, mix_across(): segment = lax.all_gather(hidden[None], 'gy', axis=0, tiled=True)  69.1 us
    all_gather x1, waiting for transfers between devices, on_device(): segment = lax.all_gather(tokens, 'gy', axis=1, tiled=True)  51.3 us
    reduce_scatter x1, waiting for transfers between devices, on_device(): lax.psum_scatter(products.astype(jnp.bfloat16), 'gy', scatter_dimension=1...  50.1 us
    all_gather x1, waiting for transfers between devices, on_device(): all_rows = lax.all_gather(rotated, 'gx', axis=0, tiled=True)  44.6 us
    dot_general x1, matrix products, on_device(): jnp.dot(segment, up_weight, preferred_element_type=jnp.float32)  27.3 us
    dot_general x1, matrix products, on_device(): jnp.dot(segment, gate_weight, preferred_element_type=jnp.float32)  22.3 us
    dot_general x1, matrix products, on_device(): jnp.dot(all_rows, down_weight, preferred_element_type=jnp.float32)  21.9 us
  transfers between devices with their start and end apart: 5, of which 5 were waited for; matrix products, arithmetic and copies ran while one was open for 0% of the time, Pallas kernels for 0%

commit v1 on v0

--- a/solution.py
+++ b/solution.py
@@ -49,7 +49,12 @@
     )
     section_two = jnp.einsum("tbd,bc->tcd", section_one, sylvester(inner_size), precision=highest)
     rotated = (section_two * factor).astype(jnp.bfloat16).reshape(row_count, col_block)
-    all_rows = lax.all_gather(rotated, "gx", axis=0, tiled=True)
+    ring = [rotated]
+    for hop in range(3):
+        ring.append(lax.ppermute(ring[-1], "gx", [(dev, (dev + 1) % 4) for dev in range(4)]))
+    all_rows = jnp.roll(
+        jnp.concatenate(ring[::-1], axis=0), (lax.axis_index("gx") + 1) * ring[0].shape[0], axis=0
+    )
     products = jnp.dot(all_rows, down_weight, preferred_element_type=jnp.float32)
     return lax.psum_scatter(products.astype(jnp.bfloat16), "gy", scatter_dimension=1, tiled=True)
 

time: 462 us -> 479 us (1.037)
  waiting for transfers between devices: 344 us -> 358 us
    ppermute x0 -> x3, waiting for transfers between devices: none -> 61.3 us  [on_device(): lax.ppermute(ring[-1], 'gx', [(dev, (dev + 1) % 4) for dev in range(4)])]
    all_gather x1 -> x0, waiting for transfers between devices: 44.6 us -> none  [on_device(): all_rows = lax.all_gather(rotated, 'gx', axis=0, tiled=True)]
  transfers between devices with their start and end apart: 5 -> 7, of which waited for: 5 -> 7; matrix products, arithmetic and copies ran while one was open for 0% -> 0% of each run, Pallas kernels for 0% -> 0%
where the time goes in v1:
time: 479 us
  waiting for transfers between devices  358 us (75%)
  matrix products  83.7 us (17%)
  other arithmetic  14 us (3%)
  between operations  13.2 us (3%)
  local copies, waits for them, and re-layouts  7.79 us (2%)
    reduce_scatter x1, waiting for transfers between devices, on_device(): lax.psum_scatter(partial_value, 'gx', scatter_dimension=0, tiled=True)  128 us
    all_gather x1, waiting for transfers between devices, mix_across(): segment = lax.all_gather(hidden[None], 'gy', axis=0, tiled=True)  69.1 us
    ppermute x3, waiting for transfers between devices, on_device(): lax.ppermute(ring[-1], 'gx', [(dev, (dev + 1) % 4) for dev in range(4)])  61.3 us
    all_gather x1, waiting for transfers between devices, on_device(): segment = lax.all_gather(tokens, 'gy', axis=1, tiled=True)  51.3 us
    reduce_scatter x1, waiting for transfers between devices, on_device(): lax.psum_scatter(products.astype(jnp.bfloat16), 'gy', scatter_dimension=1...  47.8 us
    dot_general x1, matrix products, on_device(): jnp.dot(segment, up_weight, preferred_element_type=jnp.float32)  27.3 us
    dot_general x1, matrix products, on_device(): jnp.dot(segment, gate_weight, preferred_element_type=jnp.float32)  22.3 us
    dot_general x1, matrix products, on_device(): jnp.dot(all_rows, down_weight, preferred_element_type=jnp.float32)  21.5 us
  transfers between devices with their start and end apart: 7, of which 7 were waited for; matrix products, arithmetic and copies ran while one was open for 0% of the time, Pallas kernels for 0%

profile of v1, /device:TPU:0, one launch (start us, length us, event | category | flops | bytes accessed | tf_op | source)
XLA Modules:
  0.0 479.3 jit_solution(15941951800210032179)
XLA Ops:
  6.5 0.7 all-gather.3.cloned.1.call-update
  7.3 51.3 %all-gather.3.cloned.1.call-done = bf16[512,4096]{1,0:T(8,128)(2,1)} async-done(((bf16[512,512]{1,0:T(8,128)(2,1)}), bf16[512,4096]{1,0:T(8,128)(2,1)}) %all-gather.3.cloned.1.call-update) | async-done | bytes 4194320 | tf_op jit(solution)/shard_map/all_gather | solution.py:35
  58.6 27.3 %convolution_bitcast_fusion = f32[512,1,3328]{2,0,1:T(8,128)} fusion(bf16[512,4096]{1,0:T(8,128)(2,1)} %all-gather.3.cloned.1.call-done, bf16[4096,3328]{1,0:T(8,128)(2,1)} %param.7), kind=kOutput, calls=%fused_computation.3 | convolution fusion | flops 13958643712 | bytes 38273024 | tf_op jit(solution)/shard_map/dot_general | solution.py:39
  85.9 22.3 %convolution_bitcast_fusion.1 = f32[512,1,3328]{2,0,1:T(8,128)} fusion(bf16[512,4096]{1,0:T(8,128)(2,1)S(1)} %copy-done.1, bf16[4096,3328]{1,0:T(8,128)(2,1)} %param.6), kind=kOutput, calls=%fused_computation.4 | convolution fusion | flops 13958643712 | bytes 38273024 | tf_op jit(solution)/shard_map/dot_general | solution.py:38
  108.2 10.7 %pad_maximum_fusion = f32[512,2,3328]{2,0,1:T(8,128)} fusion(f32[512,1,3328]{2,0,1:T(8,128)} %convolution_bitcast_fusion, f32[512,1,3328]{2,0,1:T(8,128)} %convolution_bitcast_fusion.1), kind=kLoop, calls=%fused_computation | loop fusion | flops 3407872 | bytes 27262976 | tf_op jit(solution)/shard_map/stack | solution.py:36
  118.9 0.0 all-gather.5.cloned.1.call-start
  118.9 128.1 %reduce-scatter.3.cloned.1.call-done = f32[128,2,3328]{2,0,1:T(8,128)} async-done(((f32[512,2,3328]{2,0,1:T(8,128)}), f32[128,2,3328]{2,0,1:T(8,128)}) %reduce-scatter.3.cloned.1.call-update) | async-done | bytes 3407888 | tf_op jit(solution)/shard_map/reduce_scatter | solution.py:43
  247.0 3.3 fusion.4
  250.4 0.0 reduce-scatter.5.cloned.1.call-start
  250.4 69.1 %all-gather.5.cloned.1.call-done = bf16[8,128,3328]{2,1,0:T(8,128)(2,1)} async-done(((bf16[1,128,3328]{2,1,0:T(8,128)(2,1)}), bf16[8,128,3328]{2,1,0:T(8,128)(2,1)}) %all-gather.5.cloned.1.call-update) | async-done | bytes 6815760 | tf_op jit(solution)/shard_map/all_gather | solution.py:22
  319.5 9.0 %fusion = f32[1,128,3328]{2,0,1:T(1,128)S(1)} fusion(bf16[8,128,3328]{2,1,0:T(8,128)(2,1)} %all-gather.5.cloned.1.call-done, s32[]{:T(128)S(6)} %axis_index.22), kind=kOutput, calls=%fused_computation.1 | convolution fusion | flops 6816256 | bytes 8519684 | tf_op jit(solution)/shard_map/dot_general | solution.py:26
  328.6 3.3 copy.11
  331.9 1.5 reshape.47
  333.3 1.7 fusion.79
  335.1 1.8 fusion.9
  336.8 0.6 copy.9
  337.4 0.2 reshape.48
  337.6 1.5 collective-permute-start
  339.1 20.5 %collective-permute-done = bf16[128,3328]{0,1:T(8,128)(2,1)S(1)} collective-permute-done((bf16[128,3328]{0,1:T(8,128)(2,1)S(1)}, bf16[128,3328]{0,1:T(8,128)(2,1)S(1)}, u32[]{:S(2)}, u32[]{:S(2)}) %collective-permute-start) | collective-permute-done | bytes 852000 | tf_op jit(solution)/shard_map/ppermute | solution.py:54
  359.6 0.6 collective-permute-start.1
  360.2 20.5 %collective-permute-done.1 = bf16[128,3328]{0,1:T(8,128)(2,1)S(1)} collective-permute-done((bf16[128,3328]{0,1:T(8,128)(2,1)S(1)}, bf16[128,3328]{0,1:T(8,128)(2,1)S(1)}, u32[]{:S(2)}, u32[]{:S(2)}) %collective-permute-start.1) | collective-permute-done | bytes 852000 | tf_op jit(solution)/shard_map/ppermute | solution.py:54
  380.7 20.3 %collective-permute-done.2 = bf16[128,3328]{0,1:T(8,128)(2,1)S(1)} collective-permute-done((bf16[128,3328]{0,1:T(8,128)(2,1)S(1)}, bf16[128,3328]{0,1:T(8,128)(2,1)S(1)}, u32[]{:S(2)}, u32[]{:S(2)}) %collective-permute-start.2) | collective-permute-done | bytes 852000 | tf_op jit(solution)/shard_map/ppermute | solution.py:54
  401.0 0.2 constant_dynamic-update-slice_fusion.7
  401.2 0.3 constant_dynamic-update-slice_fusion.6
  401.5 0.3 constant_dynamic-update-slice_fusion.5
  401.8 0.3 constant_dynamic-update-slice_fusion.4
  402.1 0.3 constant_dynamic-update-slice_fusion.3
  402.4 0.3 constant_dynamic-update-slice_fusion.2
  402.7 0.3 constant_dynamic-update-slice_fusion.1
  403.0 0.3 constant_dynamic-update-slice_fusion
  403.3 21.5 %convolution_convert_fusion = bf16[512,4096]{1,0:T(8,128)(2,1)} fusion(bf16[3328,4096]{1,0:T(8,128)(2,1)} %param.8, bf16[1024,3328]{0,1:T(8,128)(2,1)S(1)} %constant_dynamic-update-slice_fusion, s32[]{:T(128)S(6)} %select_n.14), kind=kOutput, calls=%fused_computation.5 | convolution fusion | flops 13960740864 | bytes 34865156 | tf_op jit(solution)/shard_map/dot_general | solution.py:58
  424.9 47.8 %reduce-scatter.5.cloned.1.call-done = bf16[512,512]{1,0:T(8,128)(2,1)} async-done(((bf16[512,4096]{1,0:T(8,128)(2,1)}), bf16[512,512]{1,0:T(8,128)(2,1)}) %reduce-scatter.5.cloned.1.call-update) | async-done | bytes 524304 | tf_op jit(solution)/shard_map/reduce_scatter | solution.py:59
  (10 shorter events, 0.1 us)
Async XLA Ops:
  6.5 326.8 %copy-start = (f32[52,52]{1,0:T(8,128)S(1)}, f32[52,52]{1,0:T(8,128)}, u32[]{:S(2)}) copy-start(f32[52,52]{1,0:T(8,128)} %param.9) | copy-start | bytes 32452
  6.5 52.0 %all-gather.3.cloned.1.call-start = ((), (), s32[]{:S(2)}) async-start(), calls=%async_computation.2 | async-start | bytes 4718592 | tf_op jit(solution)/shard_map/all_gather | solution.py:35
  7.3 239.8 %reduce-scatter.3.cloned.1.call-start = ((), (), s32[]{:S(2)}) async-start(), calls=%async_computation.3 | async-start | bytes 17039360 | tf_op jit(solution)/shard_map/reduce_scatter | solution.py:43
  58.6 27.3 %copy-start.1 = (bf16[512,4096]{1,0:T(8,128)(2,1)S(1)}, bf16[512,4096]{1,0:T(8,128)(2,1)}, u32[]{:S(2)}) copy-start(bf16[512,4096]{1,0:T(8,128)(2,1)} %all-gather.3.cloned.1.call-done) | copy-start | bytes 12582916
  118.9 200.7 %all-gather.5.cloned.1.call-start = ((), (), s32[]{:S(2)}) async-start(), calls=%async_computation.4 | async-start | bytes 7667712 | tf_op jit(solution)/shard_map/all_gather | solution.py:22
  250.4 222.3 %reduce-scatter.5.cloned.1.call-start = ((), (), s32[]{:S(2)}) async-start(), calls=%async_computation.5 | async-start | bytes 4718592 | tf_op jit(solution)/shard_map/reduce_scatter | solution.py:59
  337.6 22.0 %collective-permute-start = (bf16[128,3328]{0,1:T(8,128)(2,1)S(1)}, bf16[128,3328]{0,1:T(8,128)(2,1)S(1)}, u32[]{:S(2)}, u32[]{:S(2)}) collective-permute-start(bf16[128,3328]{0,1:T(8,128)(2,1)S(1)} %reshape.48), channel_id=1, source_target_pairs={{0,8},{8,16},{16,24},{24,0},{1,9},{9,17},{17,25},{25,1},{2,10},{10... | collective-permute-start | bytes 2555912 | tf_op jit(solution)/shard_map/ppermute | solution.py:54
  359.6 21.1 %collective-permute-start.1 = (bf16[128,3328]{0,1:T(8,128)(2,1)S(1)}, bf16[128,3328]{0,1:T(8,128)(2,1)S(1)}, u32[]{:S(2)}, u32[]{:S(2)}) collective-permute-start(bf16[128,3328]{0,1:T(8,128)(2,1)S(1)} %collective-permute-done), channel_id=1, source_target_pairs={{0,8},{8,16},{16,24},{24,0},{1,9},{9,17},{17,25},{25,1},{2,10},{10... | collective-permute-start | bytes 2555912 | tf_op jit(solution)/shard_map/ppermute | solution.py:54
  380.7 20.3 %collective-permute-start.2 = (bf16[128,3328]{0,1:T(8,128)(2,1)S(1)}, bf16[128,3328]{0,1:T(8,128)(2,1)S(1)}, u32[]{:S(2)}, u32[]{:S(2)}) collective-permute-start(bf16[128,3328]{0,1:T(8,128)(2,1)S(1)} %collective-permute-done.1), channel_id=1, source_target_pairs={{0,8},{8,16},{16,24},{24,0},{1,9},{9,17},{17,25},{25,1},{2,10},{10... | collective-permute-start | bytes 2555912 | tf_op jit(solution)/shard_map/ppermute | solution.py:54
Sparse Core Ops, SparseCore 0:
  8.9 49.5 all-gather.2
  119.0 127.9 reduce-scatter.2
  250.5 69.0 all-gather.4
  425.0 47.6 reduce-scatter.4
